TPU v7x, 512 devices: a whole 4x4x16 slice. The times are simulated.
512 devices in a mesh: lat: 16 (over y, x_lo, core), lon: 32 (over z, x_hi).
Axes of the slice: x: 4 (x_hi: 2, x_lo: 2; x = x_hi * 2 + x_lo), y: 4, z: 16, core: 2. Of those that a mesh axis runs over, the one named last changes fastest.
Arguments:
- queries: bfloat16 [384, 768, 128], P('lat', 'lon'), may hold values from -8 to 8
- keys: bfloat16 [384, 768, 128], P('lat', 'lon'), may hold values from -8 to 8
- values: bfloat16 [384, 768, 128], P('lat', 'lon'), may hold values from -6 to 6
- out_grad: bfloat16 [384, 768, 128], P('lat', 'lon'), may hold values from -6 to 6
Outputs:
- attended: bfloat16 [384, 768, 128], P('lat', 'lon')
- grad_queries: bfloat16 [384, 768, 128], P('lat', 'lon')
- grad_keys: bfloat16 [384, 768, 128], P('lat', 'lon')
- grad_values: bfloat16 [384, 768, 128], P('lat', 'lon')
All inputs are finite; a program needn't handle non-finite values.
Results may differ from a plain program's by a relative error of at most 0.018.
Values may be sent and summed in bfloat16 or wider, within the bound.
No kernel may reach another device: no remote copies, remote signals or barrier semaphores. Data moves between devices by JAX's collectives and lax.ppermute only.
A program may use at most 128 MiB of HBM per device.

v0:
```python
import jax
import jax.numpy as jnp
from jax import lax
from jax.experimental import pallas as pl
from jax.experimental.pallas import tpu as pltpu
from jax.sharding import PartitionSpec as P


R = 22
T = 24
W = 3 * T
BR = 8
NB = T // BR
SR = BR + 2 * R
NQ = 2 * BR * T
MID = T * W
EDGE = R * W
FAR = (SR - T) * W
PART = 2 * W
F32 = jnp.float32
BF = jnp.bfloat16
NT = (((1,), (1,)), ((), ()))
TN = (((0,), (0,)), ((), ()))


def far_base(start, b):
    return pl.multiple_of(start[b] * W, 64)


def kernel_early(start, km_ref, am_ref, q_ref, s_ref, m_ref):
    lhs = jnp.concatenate([km_ref[...], am_ref[...]], axis=1)
    s = lax.dot_general(lhs, q_ref[0], NT, preferred_element_type=F32)
    s_ref[0] = s
    m_ref[0] = jnp.max(s.reshape(MID // 8, 8, NQ), axis=0)


def kernel_a(start, kf_ref, af_ref, q_ref, g_ref, sm_ref, mm_ref, pm_ref, pf_ref, linv_ref, gs_ref, north_ref, south_ref, s_scr, m_scr, acc):
    b = pl.program_id(0)
    here = lax.rem(b, 2)
    base = far_base(start, jnp.minimum(b, NB - 1))
    prior_base = far_base(start, jnp.maximum(b - 1, 0))

    def scores(at, n, m):
        rows = pl.ds(pl.multiple_of(base + at, 16), n)
        lhs = jnp.concatenate([kf_ref[rows, :], af_ref[rows, :]], axis=1)
        s = lax.dot_general(lhs, q_ref[0], NT, preferred_element_type=F32)
        s_scr[here, pl.ds(pl.multiple_of(at, 16), n), :] = s
        return jnp.maximum(m, jnp.max(s.reshape(n // 8, 8, NQ), axis=0))

    def expo(s, p_ref, at, n, m, l):
        p = jnp.exp(s - m)
        p_ref[0, pl.ds(at, n), :] = p.astype(BF)
        return l + jnp.sum(p.reshape(n // 8, 8, NQ), axis=0)

    def expo_mid(c, l):
        at = pl.multiple_of(c * (MID // 2), 16)
        return expo(sm_ref[0, pl.ds(at, MID // 2), :], pm_ref, at, MID // 2, m_scr[:1], l)

    def expo_far(at, n, m, l):
        at = pl.multiple_of(at, 16)
        return expo(s_scr[1 - here, pl.ds(at, n), :], pf_ref, at, n, m, l)

    def close(m):
        m_scr[...] = jnp.broadcast_to(jnp.max(m, axis=0, keepdims=True), (8, NQ))

    def finish(l):
        linv = 1.0 / jnp.sum(l, axis=0, keepdims=True)
        linv_ref[0] = jnp.broadcast_to(linv, (8, NQ))
        turned = jnp.transpose(jnp.broadcast_to(linv, (128, NQ)))
        gs_ref[0] = (g_ref[0].astype(F32) * turned).astype(BF)

    zero = jnp.zeros((8, NQ), F32)

    @pl.when(b == 0)
    def _():
        acc[...] = jnp.zeros_like(acc)
        close(scores(0, FAR, mm_ref[0]))

    @pl.when((b > 0) & (b < NB))
    def _():
        m = m_scr[:1]
        l = lax.fori_loop(0, 2, expo_mid, zero)

        def both(c, carry):
            fresh, l = carry
            for i in range(7):
                fresh = scores((c * 7 + i) * PART, PART, fresh)
                l = expo_far((c * 7 + i) * PART, PART, m, l)
            return fresh, l

        fresh, l = lax.fori_loop(0, 2, both, (mm_ref[0], l))
        close(fresh)
        finish(l)

    @pl.when(b == NB)
    def _():
        m = m_scr[:1]
        l = lax.fori_loop(0, 2, expo_mid, zero)
        finish(lax.fori_loop(0, 2, lambda c, l: expo_far(c * (FAR // 2), FAR // 2, m, l), l))

    @pl.when(b > 0)
    def _():
        acc[pl.ds(prior_base, FAR), :] += jnp.dot(pf_ref[0], gs_ref[0], preferred_element_type=F32)

    @pl.when(b == NB)
    def _():
        north_ref[...] = acc[:EDGE, :].astype(BF)
        south_ref[...] = acc[EDGE:, :].astype(BF)


def score_grads(p, v, gs, corr):
    gw = lax.dot_general(v, gs, NT, preferred_element_type=F32)
    return (p.astype(F32) * (gw - corr)).astype(BF)


def kernel_far(start, vm_ref, vf_ref, q_ref, gs_ref, pm_ref, pf_ref, linv_ref, o_ref, corr_ref, ds_ref, north_ref, south_ref, acc):
    b = pl.program_id(0)
    rows = pl.ds(far_base(start, b), FAR)

    @pl.when(b == 0)
    def _():
        acc[...] = jnp.zeros_like(acc)

    gs = gs_ref[0]
    ot = lax.dot_general(vm_ref[...], pm_ref[0], TN, preferred_element_type=F32)
    ot += lax.dot_general(vf_ref[rows, :], pf_ref[0], TN, preferred_element_type=F32)
    lane = lax.broadcasted_iota(jnp.int32, (NQ // 2, 128), 1)
    o = jnp.transpose(ot * linv_ref[0][:1])
    o_ref[...] = jnp.where(lane < 64, o[: NQ // 2], o[NQ // 2 :]).astype(BF)
    row = jnp.sum(gs.astype(F32) * o.astype(BF).astype(F32), axis=1, keepdims=True)
    corr = jnp.transpose(jnp.broadcast_to(row, (NQ, 128)))
    corr_ref[0] = corr[:8]
    ds = score_grads(pf_ref[0], vf_ref[rows, :], gs, corr[:1])
    ds_ref[0] = ds
    acc[rows, :] += jnp.dot(ds, q_ref[0][:, :128], preferred_element_type=F32)

    @pl.when(b == NB - 1)
    def _():
        north_ref[...] = acc[:EDGE, :].astype(BF)
        south_ref[...] = acc[EDGE:, :].astype(BF)


def kernel_mid(start, km_ref, kf_ref, vm_ref, q_ref, gs_ref, pm_ref, corr_ref, ds_ref, dq_ref, grads_ref):
    b = pl.program_id(0)

    @pl.when(b == 0)
    def _():
        grads_ref[...] = jnp.zeros_like(grads_ref)

    gs = gs_ref[0]
    ds = score_grads(pm_ref[0], vm_ref[...], gs, corr_ref[0][:1])
    grads_ref[0] += jnp.dot(ds, q_ref[0][:, :128], preferred_element_type=F32)
    dqt = lax.dot_general(km_ref[...], ds, TN, preferred_element_type=F32)
    dqt += lax.dot_general(kf_ref[pl.ds(far_base(start, b), FAR), :], ds_ref[0], TN, preferred_element_type=F32)
    grads_ref[1] += jnp.dot(pm_ref[0], gs, preferred_element_type=F32)
    lane = lax.broadcasted_iota(jnp.int32, (NQ // 2, 128), 1)
    dq = jnp.transpose(dqt * 0.125)
    dq_ref[...] = jnp.where(lane < 64, dq[: NQ // 2], dq[NQ // 2 :]).astype(BF)


def whole(*shape):
    return pl.BlockSpec(shape, lambda b, s: (0,) * len(shape))


def per_block(*shape, at=lambda b: b):
    return pl.BlockSpec((1,) + shape, lambda b, s: (at(b),) + (0,) * len(shape))


def rows_of_block():
    return pl.BlockSpec((NQ // 2, 128), lambda b, s: (b, 0))


def sds(*shape, dtype=BF):
    return jax.ShapeDtypeStruct(shape, dtype)


def call(kernel, grid, in_specs, out_specs, out_shape, scratch, flops):
    return pl.pallas_call(
        kernel,
        grid_spec=pltpu.PrefetchScalarGridSpec(
            num_scalar_prefetch=1, grid=(grid,), in_specs=in_specs, out_specs=out_specs, scratch_shapes=scratch
        ),
        out_shape=out_shape,
        compiler_params=pltpu.CompilerParams(vmem_limit_bytes=24 << 20),
        cost_estimate=pl.CostEstimate(flops=flops, bytes_accessed=14_000_000, transcendentals=0),
    )


def run_early(start, km, am, q):
    return call(
        kernel_early,
        NB,
        [whole(MID, 128), whole(MID, 128), per_block(NQ, 256)],
        [per_block(MID, NQ), per_block(8, NQ)],
        [sds(NB, MID, NQ, dtype=F32), sds(NB, 8, NQ, dtype=F32)],
        [],
        1_000_000_000,
    )(start, km, am, q)


def run_a(start, kf, af, q, g, sm, mm):
    ahead = lambda b: jnp.minimum(b, NB - 1)
    behind = lambda b: jnp.maximum(b - 1, 0)
    return call(
        kernel_a,
        NB + 1,
        [whole(2 * EDGE, 128), whole(2 * EDGE, 128), per_block(NQ, 256, at=ahead), per_block(NQ, 128, at=behind)]
        + [per_block(MID, NQ, at=behind), per_block(8, NQ, at=ahead)],
        [per_block(*x, at=behind) for x in ((MID, NQ), (FAR, NQ), (8, NQ), (NQ, 128))] + [whole(EDGE, 128)] * 2,
        [sds(NB, MID, NQ), sds(NB, FAR, NQ), sds(NB, 8, NQ, dtype=F32), sds(NB, NQ, 128)] + [sds(EDGE, 128)] * 2,
        [pltpu.VMEM((2, FAR, NQ), F32), pltpu.VMEM((8, NQ), F32), pltpu.VMEM((2 * EDGE, 128), F32)],
        5_000_000_000,
    )(start, kf, af, q, g, sm, mm)


def run_far(start, vm, vf, q, gs, pm, pf, linv):
    return call(
        kernel_far,
        NB,
        [whole(MID, 128), whole(2 * EDGE, 128), per_block(NQ, 256), per_block(NQ, 128)]
        + [per_block(MID, NQ), per_block(FAR, NQ), per_block(8, NQ)],
        [rows_of_block(), per_block(8, NQ), per_block(FAR, NQ)] + [whole(EDGE, 128)] * 2,
        [sds(T * T, 128), sds(NB, 8, NQ, dtype=F32), sds(NB, FAR, NQ)] + [sds(EDGE, 128)] * 2,
        [pltpu.VMEM((2 * EDGE, 128), F32)],
        5_000_000_000,
    )(start, vm, vf, q, gs, pm, pf, linv)


def run_mid(start, km, kf, vm, q, gs, pm, corr, ds):
    return call(
        kernel_mid,
        NB,
        [whole(MID, 128), whole(2 * EDGE, 128), whole(MID, 128), per_block(NQ, 256), per_block(NQ, 128)]
        + [per_block(MID, NQ), per_block(8, NQ), per_block(FAR, NQ)],
        [rows_of_block(), whole(2, MID, 128)],
        [sds(T * T, 128), sds(2, MID, 128, dtype=F32)],
        [],
        5_000_000_000,
    )(start, km, kf, vm, q, gs, pm, corr, ds)


def tables(first_row, height):
    i0 = first_row + BR * jnp.arange(NB, dtype=jnp.int32)
    f0 = jnp.clip(i0 - R, 0, height - 45)
    start = jnp.clip(f0 - first_row + R, 0, T - BR) // 8 * 8

    def lanes(krow, n):
        krow = krow + (first_row - R)
        kcol = lax.broadcasted_iota(jnp.int32, (n, W, 128), 1)
        lane = lax.broadcasted_iota(jnp.int32, (n, W, 128), 2)
        f = jnp.clip(first_row + lane - R, 0, height - 45)
        row_out = (lane < T) & ((krow < f) | (krow >= f + 45))
        qcol = lane - T
        col_out = (lane >= T) & (lane < 2 * T) & ((kcol < qcol + 2) | (kcol > qcol + 46))
        return jnp.where(row_out | col_out, -1e30, 0.0).astype(BF).reshape(n * W, 128)

    far = lax.broadcasted_iota(jnp.int32, (2 * R, W, 128), 0)
    mid = lax.broadcasted_iota(jnp.int32, (T, W, 128), 0) + R
    return start.astype(jnp.int32), lanes(mid, T), lanes(far + jnp.where(far >= R, T, 0), 2 * R)


def spread(x, scale):
    x = (x.reshape(NB, 1, BR * T, 128) * scale).astype(BF)
    lane = lax.broadcasted_iota(jnp.int32, (1, 2, 1, 128), 3) // 64
    head = lax.broadcasted_iota(jnp.int32, (1, 2, 1, 128), 1)
    return jnp.where(lane == head, x, jnp.zeros((), BF)).reshape(NB, NQ, 128)


def with_marks(q):
    lane = lax.broadcasted_iota(jnp.int32, (NB, 2, BR, T, 128), 4)
    row = lax.broadcasted_iota(jnp.int32, (NB, 2, BR, T, 128), 0) * BR + lax.broadcasted_iota(jnp.int32, (NB, 2, BR, T, 128), 2)
    col = lax.broadcasted_iota(jnp.int32, (NB, 2, BR, T, 128), 3)
    mark = jnp.where((lane == row) | (lane == T + col), 1.0, 0.0).astype(BF).reshape(NB, NQ, 128)
    return jnp.concatenate([spread(q, 0.125), mark], axis=2)


def shift(x, by):
    n = lax.axis_size("lat")
    return lax.ppermute(x, "lat", [(i, i + by) for i in range(n) if 0 <= i + by < n])


def swap(x, first):
    n = lax.axis_size("lon")
    pairs = [(i % n, (i + 1) % n) for i in range(first, n + first, 2)]
    return lax.ppermute(x, "lon", pairs + [(b, a) for a, b in pairs])


def far_rows(mid):
    return jnp.concatenate([shift(mid[T - R :], 1), shift(mid[:R], -1)], axis=0).reshape(2 * EDGE, 128)


def from_lat(north, south):
    from_south = shift(north, -1).reshape(R, W, 128).astype(F32)
    from_north = shift(south, 1).reshape(R, W, 128).astype(F32)
    pad = ((T - R, 0), (0, 0), (0, 0)), ((0, T - R), (0, 0), (0, 0))
    return jnp.pad(from_south, pad[0]) + jnp.pad(from_north, pad[1])


def body(queries, keys, values, out_grad):
    height = T * lax.axis_size("lat")
    even = lax.axis_index("lon") % 2 == 0
    start, am, af = tables(lax.axis_index("lat") * T, height)
    q = with_marks(queries)
    g = spread(out_grad, 1.0)
    pair = jnp.stack([keys, values])
    near = swap(pair, 0)
    far = swap(pair, 1)

    def widen(x, i):
        return jnp.concatenate([jnp.where(even, far[i], near[i]), x, jnp.where(even, near[i], far[i])], axis=1)

    km = widen(keys, 0)
    vm = widen(values, 1)
    kf = far_rows(km)
    vf = far_rows(vm)
    km = km.reshape(MID, 128)
    vm = vm.reshape(MID, 128)
    sm, mm = run_early(start, km, am, q)
    pm, pf, linv, gs, *dvf = run_a(start, kf, af, q, g, sm, mm)
    dvf = from_lat(*dvf)
    attended, corr, ds, *dkf = run_far(start, vm, vf, q, gs, pm, pf, linv)
    dkf = from_lat(*dkf)
    grad_queries, mid = run_mid(start, km, kf, vm, q, gs, pm, corr, ds)
    mid = mid.reshape(2, T, W, 128) + jnp.stack([dkf, dvf])
    west = mid[:, :, :T].astype(BF)
    east = mid[:, :, 2 * T :].astype(BF)
    near = swap(jnp.where(even, east, west), 0)
    far = swap(jnp.where(even, west, east), 1)
    grads = [(mid[i, :, T : 2 * T] + near[i].astype(F32) + far[i].astype(F32)).astype(BF) for i in range(2)]
    return attended.reshape(T, T, 128), grad_queries.reshape(T, T, 128), grads[0], grads[1]


def solution(mesh):
    spec = P("lat", "lon", None)
    return jax.shard_map(body, mesh=mesh, in_specs=(spec,) * 4, out_specs=(spec,) * 4, check_vma=False)
```

profile of v0, /device:TPU:18, one launch (start us, length us, event | category | flops | bytes accessed | tf_op | source)
XLA Modules:
  0.0 103.9 jit_solution(16848542638695664510)
XLA Ops:
  0.6 1.0 pad_maximum_fusion.5
  1.6 13.0 %collective-permute-start = (bf16[2,24,24,128]{3,2,1,0:T(8,128)(2,1)S(1)}, bf16[2,24,24,128]{3,2,1,0:T(8,128)(2,1)S(1)}, u32[]{:S(2)}, u32[]{:S(2)}) collective-permute-start(bf16[2,24,24,128]{3,2,1,0:T(8,128)(2,1)S(1)} %pad_maximum_fusion.5), channel_id=1, source_target_pairs={{1,2},{3,4},{5,6},{7,8},{9,10},{11,12},{13,14},{15,16},{17,18},{19... | collective-permute-start | bytes 884744 | tf_op jit(solution)/shard_map/ppermute | solution.py:285
  14.6 1.9 %collective-permute-start.1 = (bf16[2,24,24,128]{3,2,1,0:T(8,128)(2,1)S(1)}, bf16[2,24,24,128]{3,2,1,0:T(8,128)(2,1)S(1)}, u32[]{:S(2)}, u32[]{:S(2)}) collective-permute-start(bf16[2,24,24,128]{3,2,1,0:T(8,128)(2,1)S(1)} %pad_maximum_fusion.5), channel_id=1, source_target_pairs={{0,1},{2,3},{4,5},{6,7},{8,9},{10,11},{12,13},{14,15},{16,17},{18,... | collective-permute-start | bytes 884744 | tf_op jit(solution)/shard_map/ppermute | solution.py:285
  18.4 1.0 bitcast_select_fusion
  19.6 1.8 %select_convert_fusion.af_ref = bf16[3168,128]{1,0:T(8,128)(2,1)S(1)} fusion(s32[128]{0:T(128)S(1)} %get-tuple-element.59, s32[128]{0:T(128)S(1)} %get-tuple-element.58, s32[128]{0:T(128)S(1)} %get-tuple-element.51, s32[128]{0:T(128)S(1)} %get-tuple-element.50, s32[3168]{0:T(1024)S(1)} %iota.176, s32[3168]{0:T(1024)S(1)} %add.159, ...), kind=kLoop, calls=%fused_computation.1 | loop fusion | flops 4460544 | bytes 838656 | tf_op jit(solution)/shard_map/convert_element_type | solution.py:255
  21.5 1.1 %select_convert_fusion.1.am_ref = bf16[1728,128]{1,0:T(8,128)(2,1)S(1)} fusion(s32[128]{0:T(128)S(1)} %get-tuple-element.59, s32[128]{0:T(128)S(1)} %get-tuple-element.58, s32[128]{0:T(128)S(1)} %get-tuple-element.51, s32[128]{0:T(128)S(1)} %get-tuple-element.50, s32[1728]{0:T(1024)S(1)} %iota.188, s32[1728]{0:T(1024)S(1)} %add.170, ...), kind=kLoop, calls=%fused_computation.4 | loop fusion | flops 2433024 | bytes 458496 | tf_op jit(solution)/shard_map/convert_element_type | solution.py:255
  22.6 5.4 %collective-permute-done.1 = bf16[2,24,24,128]{3,2,1,0:T(8,128)(2,1)S(1)} collective-permute-done((bf16[2,24,24,128]{3,2,1,0:T(8,128)(2,1)S(1)}, bf16[2,24,24,128]{3,2,1,0:T(8,128)(2,1)S(1)}, u32[]{:S(2)}, u32[]{:S(2)}) %collective-permute-start.1) | collective-permute-done | bytes 294944 | tf_op jit(solution)/shard_map/ppermute | solution.py:285
  28.2 1.9 %collective-permute-start.4 = (bf16[22,72,128]{2,1,0:T(8,128)(2,1)S(1)}, bf16[22,72,128]{2,1,0:T(8,128)(2,1)S(1)}, u32[]{:S(2)}, u32[]{:S(2)}) collective-permute-start(bf16[22,72,128]{2,1,0:T(8,128)(2,1)S(1)} %get-tuple-element.44), channel_id=1, source_target_pairs={{0,32},{32,64},{64,96},{96,128},{128,160},{160,192},{192,224},{224... | collective-permute-start | bytes 1216520 | tf_op jit(solution)/shard_map/ppermute | solution.py:279
  30.1 3.6 %collective-permute-start.5 = (bf16[22,72,128]{2,1,0:T(8,128)(2,1)S(1)}, bf16[22,72,128]{2,1,0:T(8,128)(2,1)S(1)}, u32[]{:S(2)}, u32[]{:S(2)}) collective-permute-start(bf16[22,72,128]{2,1,0:T(8,128)(2,1)S(1)} %get-tuple-element.45), channel_id=1, source_target_pairs={{32,0},{64,32},{96,64},{128,96},{160,128},{192,160},{224,192},{256... | collective-permute-start | bytes 1216520 | tf_op jit(solution)/shard_map/ppermute | solution.py:279
  33.9 2.4 %collective-permute-start.2 = (bf16[22,72,128]{2,1,0:T(8,128)(2,1)S(1)}, bf16[22,72,128]{2,1,0:T(8,128)(2,1)S(1)}, u32[]{:S(2)}, u32[]{:S(2)}) collective-permute-start(bf16[22,72,128]{2,1,0:T(8,128)(2,1)S(1)} %get-tuple-element.46), channel_id=1, source_target_pairs={{0,32},{32,64},{64,96},{96,128},{128,160},{160,192},{192,224},{224... | collective-permute-start | bytes 1216520 | tf_op jit(solution)/shard_map/ppermute | solution.py:279
  36.4 3.1 %collective-permute-start.3 = (bf16[22,72,128]{2,1,0:T(8,128)(2,1)S(1)}, bf16[22,72,128]{2,1,0:T(8,128)(2,1)S(1)}, u32[]{:S(2)}, u32[]{:S(2)}) collective-permute-start(bf16[22,72,128]{2,1,0:T(8,128)(2,1)S(1)} %get-tuple-element.47), channel_id=1, source_target_pairs={{32,0},{64,32},{96,64},{128,96},{160,128},{192,160},{224,192},{256... | collective-permute-start | bytes 1216520 | tf_op jit(solution)/shard_map/ppermute | solution.py:279
  39.5 2.5 %shard_map.75 = (f32[3,1728,384]{2,1,0:T(8,128)S(1)}, f32[3,8,384]{2,1,0:T(8,128)S(1)}) custom-call(s32[3]{0:T(128)S(1)} %fusion.7.start, bf16[1728,128]{1,0:T(8,128)(2,1)S(1)} %bitcast.38, bf16[1728,128]{1,0:T(8,128)(2,1)S(1)} %select_convert_fusion.1.am_ref, bf16[3,384,256]{2,1,0:T(8,128)(2,1)S(1)} %pad_maximum_fusion.2.q_ref), custom_call_target="tpu_custom_call" | custom-call | flops 1000000000 | bytes 14000000 | tf_op jit(solution)/shard_map/pallas_call | solution.py:190
  42.0 1.5 %collective-permute-done.5 = bf16[22,72,128]{2,1,0:T(8,128)(2,1)S(1)} collective-permute-done((bf16[22,72,128]{2,1,0:T(8,128)(2,1)S(1)}, bf16[22,72,128]{2,1,0:T(8,128)(2,1)S(1)}, u32[]{:S(2)}, u32[]{:S(2)}) %collective-permute-start.5) | collective-permute-done | bytes 405536 | tf_op jit(solution)/shard_map/ppermute | solution.py:279
  43.6 8.0 %shard_map.76 = (bf16[3,1728,384]{2,1,0:T(8,128)(2,1)S(1)}, bf16[3,2016,384]{2,1,0:T(8,128)(2,1)S(1)}, f32[3,8,384]{2,1,0:T(8,128)S(1)}, bf16[3,384,128]{2,1,0:T...) custom-call(s32[3]{0:T(128)S(1)} %fusion.7.start, bf16[3168,128]{1,0:T(8,128)(2,1)S(1)} %bitcast.41, ...), custom_call_target="tpu_custom_call" | custom-call | flops 5000000000 | bytes 14000000 | tf_op jit(solution)/shard_map/pallas_call | solution.py:204
  51.7 7.5 %shard_map.77 = (bf16[576,128]{1,0:T(8,128)(2,1)}, f32[3,8,384]{2,1,0:T(8,128)S(1)}, bf16[3,2016,384]{2,1,0:T(8,128)(2,1)S(1)}, bf16[1584,128]{1,0:T(8,128)(2,1)S(1)}, bf16[1584,128]{1,0:T(8,128)(2,1)S(1)}) custom-call(s32[3]{0:T(128)S(1)} %fusion.7.start, bf16[1728,128]{1,0:T(8,128)(2,1)S(1)} %bitcast.36, bf16[3168,128]{1,0:T(8,128)(2,1)S(1)} %bitcast.43, ...), custom_call_target="tpu_custom_call" | custom-call | flops 5000000000 | bytes 14000000 | tf_op jit(solution)/shard_map/pallas_call | solution.py:217
  59.2 4.1 %collective-permute-start.6 = (bf16[1584,128]{1,0:T(8,128)(2,1)S(1)}, bf16[1584,128]{1,0:T(8,128)(2,1)S(1)}, u32[]{:S(2)}, u32[]{:S(2)}) collective-permute-start(bf16[1584,128]{1,0:T(8,128)(2,1)S(1)} %get-tuple-element.30), channel_id=1, source_target_pairs={{32,0},{64,32},{96,64},{128,96},{160,128},{192,160},{224,192},{256... | collective-permute-start | bytes 1216520 | tf_op jit(solution)/shard_map/ppermute | solution.py:279
  63.3 1.9 %collective-permute-start.7 = (bf16[1584,128]{1,0:T(8,128)(2,1)S(1)}, bf16[1584,128]{1,0:T(8,128)(2,1)S(1)}, u32[]{:S(2)}, u32[]{:S(2)}) collective-permute-start(bf16[1584,128]{1,0:T(8,128)(2,1)S(1)} %get-tuple-element.31), channel_id=1, source_target_pairs={{0,32},{32,64},{64,96},{96,128},{128,160},{160,192},{192,224},{224... | collective-permute-start | bytes 1216520 | tf_op jit(solution)/shard_map/ppermute | solution.py:279
  65.2 3.6 %collective-permute-start.8 = (bf16[1584,128]{1,0:T(8,128)(2,1)S(1)}, bf16[1584,128]{1,0:T(8,128)(2,1)S(1)}, u32[]{:S(2)}, u32[]{:S(2)}) collective-permute-start(bf16[1584,128]{1,0:T(8,128)(2,1)S(1)} %get-tuple-element.32), channel_id=1, source_target_pairs={{32,0},{64,32},{96,64},{128,96},{160,128},{192,160},{224,192},{256... | collective-permute-start | bytes 1216520 | tf_op jit(solution)/shard_map/ppermute | solution.py:279
  68.8 2.8 %collective-permute-start.9 = (bf16[1584,128]{1,0:T(8,128)(2,1)S(1)}, bf16[1584,128]{1,0:T(8,128)(2,1)S(1)}, u32[]{:S(2)}, u32[]{:S(2)}) collective-permute-start(bf16[1584,128]{1,0:T(8,128)(2,1)S(1)} %get-tuple-element.33), channel_id=1, source_target_pairs={{0,32},{32,64},{64,96},{96,128},{128,160},{160,192},{192,224},{224... | collective-permute-start | bytes 1216520 | tf_op jit(solution)/shard_map/ppermute | solution.py:279
  71.6 6.7 %shard_map.78 = (bf16[576,128]{1,0:T(8,128)(2,1)}, f32[2,1728,128]{2,1,0:T(8,128)S(1)}) custom-call(s32[3]{0:T(128)S(1)} %fusion.7.start, bf16[1728,128]{1,0:T(8,128)(2,1)S(1)} %bitcast.39, bf16[3168,128]{1,0:T(8,128)(2,1)S(1)} %bitcast.42, bf16[1728,128]{1,0:T(8,128)(2,1)S(1)} %bitcast.37, bf16[3,384,256]{2,1,0:T(8,128)(2,1)S(1)} %pad_maximum_fusion.2.q_ref, ...), custom_call_target="tpu_custom_call" | custom-call | flops 5000000000 | bytes 14000000 | tf_op jit(solution)/shard_map/pallas_call | solution.py:230
  78.6 5.3 %collective-permute-done.9 = bf16[1584,128]{1,0:T(8,128)(2,1)S(1)} collective-permute-done((bf16[1584,128]{1,0:T(8,128)(2,1)S(1)}, bf16[1584,128]{1,0:T(8,128)(2,1)S(1)}, u32[]{:S(2)}, u32[]{:S(2)}) %collective-permute-start.9) | collective-permute-done | bytes 405536 | tf_op jit(solution)/shard_map/ppermute | solution.py:279
  84.4 1.9 %collective-permute-start.10 = (bf16[2,24,24,128]{3,2,1,0:T(8,128)(2,1)S(1)}, bf16[2,24,24,128]{3,2,1,0:T(8,128)(2,1)S(1)}, u32[]{:S(2)}, u32[]{:S(2)}) collective-permute-start(bf16[2,24,24,128]{3,2,1,0:T(8,128)(2,1)S(1)} %get-tuple-element.38), channel_id=1, source_target_pairs={{0,1},{2,3},{4,5},{6,7},{8,9},{10,11},{12,13},{14,15},{16,17},{18,... | collective-permute-start | bytes 884744 | tf_op jit(solution)/shard_map/ppermute | solution.py:285
  86.3 7.0 %collective-permute-start.11 = (bf16[2,24,24,128]{3,2,1,0:T(8,128)(2,1)S(1)}, bf16[2,24,24,128]{3,2,1,0:T(8,128)(2,1)S(1)}, u32[]{:S(2)}, u32[]{:S(2)}) collective-permute-start(bf16[2,24,24,128]{3,2,1,0:T(8,128)(2,1)S(1)} %get-tuple-element.39), channel_id=1, source_target_pairs={{1,2},{3,4},{5,6},{7,8},{9,10},{11,12},{13,14},{15,16},{17,18},{19... | collective-permute-start | bytes 884744 | tf_op jit(solution)/shard_map/ppermute | solution.py:285
  93.3 9.8 %collective-permute-done.10 = bf16[2,24,24,128]{3,2,1,0:T(8,128)(2,1)S(1)} collective-permute-done((bf16[2,24,24,128]{3,2,1,0:T(8,128)(2,1)S(1)}, bf16[2,24,24,128]{3,2,1,0:T(8,128)(2,1)S(1)}, u32[]{:S(2)}, u32[]{:S(2)}) %collective-permute-start.10) | collective-permute-done | bytes 294944 | tf_op jit(solution)/shard_map/ppermute | solution.py:285
  (50 shorter events, 3.9 us)
Async XLA Ops:
  1.6 20.9 %collective-permute-start = (bf16[2,24,24,128]{3,2,1,0:T(8,128)(2,1)S(1)}, bf16[2,24,24,128]{3,2,1,0:T(8,128)(2,1)S(1)}, u32[]{:S(2)}, u32[]{:S(2)}) collective-permute-start(bf16[2,24,24,128]{3,2,1,0:T(8,128)(2,1)S(1)} %pad_maximum_fusion.5), channel_id=1, source_target_pairs={{1,2},{3,4},{5,6},{7,8},{9,10},{11,12},{13,14},{15,16},{17,18},{19... | collective-permute-start | bytes 884744 | tf_op jit(solution)/shard_map/ppermute | solution.py:285
  14.6 13.3 %collective-permute-start.1 = (bf16[2,24,24,128]{3,2,1,0:T(8,128)(2,1)S(1)}, bf16[2,24,24,128]{3,2,1,0:T(8,128)(2,1)S(1)}, u32[]{:S(2)}, u32[]{:S(2)}) collective-permute-start(bf16[2,24,24,128]{3,2,1,0:T(8,128)(2,1)S(1)} %pad_maximum_fusion.5), channel_id=1, source_target_pairs={{0,1},{2,3},{4,5},{6,7},{8,9},{10,11},{12,13},{14,15},{16,17},{18,... | collective-permute-start | bytes 884744 | tf_op jit(solution)/shard_map/ppermute | solution.py:285
  19.5 8.5 %copy-start = (bf16[24,24,128]{2,1,0:T(8,128)(2,1)S(1)}, bf16[24,24,128]{2,1,0:T(8,128)(2,1)}, u32[]{:S(2)}) copy-start(bf16[24,24,128]{2,1,0:T(8,128)(2,1)} %param.6) | copy-start | bytes 442372
  19.5 8.5 %copy-start.1 = (bf16[24,24,128]{2,1,0:T(8,128)(2,1)S(1)}, bf16[24,24,128]{2,1,0:T(8,128)(2,1)}, u32[]{:S(2)}) copy-start(bf16[24,24,128]{2,1,0:T(8,128)(2,1)} %param.5) | copy-start | bytes 442372
  28.2 13.8 %collective-permute-start.4 = (bf16[22,72,128]{2,1,0:T(8,128)(2,1)S(1)}, bf16[22,72,128]{2,1,0:T(8,128)(2,1)S(1)}, u32[]{:S(2)}, u32[]{:S(2)}) collective-permute-start(bf16[22,72,128]{2,1,0:T(8,128)(2,1)S(1)} %get-tuple-element.44), channel_id=1, source_target_pairs={{0,32},{32,64},{64,96},{96,128},{128,160},{160,192},{192,224},{224... | collective-permute-start | bytes 1216520 | tf_op jit(solution)/shard_map/ppermute | solution.py:279
  30.1 13.4 %collective-permute-start.5 = (bf16[22,72,128]{2,1,0:T(8,128)(2,1)S(1)}, bf16[22,72,128]{2,1,0:T(8,128)(2,1)S(1)}, u32[]{:S(2)}, u32[]{:S(2)}) collective-permute-start(bf16[22,72,128]{2,1,0:T(8,128)(2,1)S(1)} %get-tuple-element.45), channel_id=1, source_target_pairs={{32,0},{64,32},{96,64},{128,96},{160,128},{192,160},{224,192},{256... | collective-permute-start | bytes 1216520 | tf_op jit(solution)/shard_map/ppermute | solution.py:279
  33.9 17.7 %collective-permute-start.2 = (bf16[22,72,128]{2,1,0:T(8,128)(2,1)S(1)}, bf16[22,72,128]{2,1,0:T(8,128)(2,1)S(1)}, u32[]{:S(2)}, u32[]{:S(2)}) collective-permute-start(bf16[22,72,128]{2,1,0:T(8,128)(2,1)S(1)} %get-tuple-element.46), channel_id=1, source_target_pairs={{0,32},{32,64},{64,96},{96,128},{128,160},{160,192},{192,224},{224... | collective-permute-start | bytes 1216520 | tf_op jit(solution)/shard_map/ppermute | solution.py:279
  36.4 15.2 %collective-permute-start.3 = (bf16[22,72,128]{2,1,0:T(8,128)(2,1)S(1)}, bf16[22,72,128]{2,1,0:T(8,128)(2,1)S(1)}, u32[]{:S(2)}, u32[]{:S(2)}) collective-permute-start(bf16[22,72,128]{2,1,0:T(8,128)(2,1)S(1)} %get-tuple-element.47), channel_id=1, source_target_pairs={{32,0},{64,32},{96,64},{128,96},{160,128},{192,160},{224,192},{256... | collective-permute-start | bytes 1216520 | tf_op jit(solution)/shard_map/ppermute | solution.py:279
  59.2 19.2 %collective-permute-start.6 = (bf16[1584,128]{1,0:T(8,128)(2,1)S(1)}, bf16[1584,128]{1,0:T(8,128)(2,1)S(1)}, u32[]{:S(2)}, u32[]{:S(2)}) collective-permute-start(bf16[1584,128]{1,0:T(8,128)(2,1)S(1)} %get-tuple-element.30), channel_id=1, source_target_pairs={{32,0},{64,32},{96,64},{128,96},{160,128},{192,160},{224,192},{256... | collective-permute-start | bytes 1216520 | tf_op jit(solution)/shard_map/ppermute | solution.py:279
  63.3 15.1 %collective-permute-start.7 = (bf16[1584,128]{1,0:T(8,128)(2,1)S(1)}, bf16[1584,128]{1,0:T(8,128)(2,1)S(1)}, u32[]{:S(2)}, u32[]{:S(2)}) collective-permute-start(bf16[1584,128]{1,0:T(8,128)(2,1)S(1)} %get-tuple-element.31), channel_id=1, source_target_pairs={{0,32},{32,64},{64,96},{96,128},{128,160},{160,192},{192,224},{224... | collective-permute-start | bytes 1216520 | tf_op jit(solution)/shard_map/ppermute | solution.py:279
  65.2 13.4 %collective-permute-start.8 = (bf16[1584,128]{1,0:T(8,128)(2,1)S(1)}, bf16[1584,128]{1,0:T(8,128)(2,1)S(1)}, u32[]{:S(2)}, u32[]{:S(2)}) collective-permute-start(bf16[1584,128]{1,0:T(8,128)(2,1)S(1)} %get-tuple-element.32), channel_id=1, source_target_pairs={{32,0},{64,32},{96,64},{128,96},{160,128},{192,160},{224,192},{256... | collective-permute-start | bytes 1216520 | tf_op jit(solution)/shard_map/ppermute | solution.py:279
  68.8 15.1 %collective-permute-start.9 = (bf16[1584,128]{1,0:T(8,128)(2,1)S(1)}, bf16[1584,128]{1,0:T(8,128)(2,1)S(1)}, u32[]{:S(2)}, u32[]{:S(2)}) collective-permute-start(bf16[1584,128]{1,0:T(8,128)(2,1)S(1)} %get-tuple-element.33), channel_id=1, source_target_pairs={{0,32},{32,64},{64,96},{96,128},{128,160},{160,192},{192,224},{224... | collective-permute-start | bytes 1216520 | tf_op jit(solution)/shard_map/ppermute | solution.py:279
  84.4 18.7 %collective-permute-start.10 = (bf16[2,24,24,128]{3,2,1,0:T(8,128)(2,1)S(1)}, bf16[2,24,24,128]{3,2,1,0:T(8,128)(2,1)S(1)}, u32[]{:S(2)}, u32[]{:S(2)}) collective-permute-start(bf16[2,24,24,128]{3,2,1,0:T(8,128)(2,1)S(1)} %get-tuple-element.38), channel_id=1, source_target_pairs={{0,1},{2,3},{4,5},{6,7},{8,9},{10,11},{12,13},{14,15},{16,17},{18,... | collective-permute-start | bytes 884744 | tf_op jit(solution)/shard_map/ppermute | solution.py:285
  86.3 16.8 %collective-permute-start.11 = (bf16[2,24,24,128]{3,2,1,0:T(8,128)(2,1)S(1)}, bf16[2,24,24,128]{3,2,1,0:T(8,128)(2,1)S(1)}, u32[]{:S(2)}, u32[]{:S(2)}) collective-permute-start(bf16[2,24,24,128]{3,2,1,0:T(8,128)(2,1)S(1)} %get-tuple-element.39), channel_id=1, source_target_pairs={{1,2},{3,4},{5,6},{7,8},{9,10},{11,12},{13,14},{15,16},{17,18},{19... | collective-permute-start | bytes 884744 | tf_op jit(solution)/shard_map/ppermute | solution.py:285
where the time goes:
time: 104 us
  starting transfers between devices  47.4 us (46%)
  Pallas kernels  24.7 us (24%)
  waiting for transfers between devices  22 us (21%)
  other arithmetic  7.84 us (8%)
  between operations  1.07 us (1%)
    ppermute x4, starting transfers between devices, swap(): return lax.ppermute(x, 'lon', pairs + [(b, a) for a, b in pairs])  23.8 us
    ppermute x8, starting transfers between devices, shift(): lax.ppermute(x, 'lat', [(i, i + by) for i in range(n) if 0 <= i + by < n])  23.6 us
    ppermute x4, waiting for transfers between devices, swap(): return lax.ppermute(x, 'lon', pairs + [(b, a) for a, b in pairs])  15.1 us
    pallas_call x1, Pallas kernels, run_a(): call(kernel_a, NB + 1, [whole(2 * EDGE, 128), whole(2 * EDGE, 128), per_b...  7.97 us
    pallas_call x1, Pallas kernels, run_far(): call(kernel_far, NB, [whole(MID, 128), whole(2 * EDGE, 128), per_block(NQ...  7.48 us
    ppermute x8, waiting for transfers between devices, shift(): lax.ppermute(x, 'lat', [(i, i + by) for i in range(n) if 0 <= i + by < n])  6.93 us
    pallas_call x1, Pallas kernels, run_mid(): call(kernel_mid, NB, [whole(MID, 128), whole(2 * EDGE, 128), whole(MID, 1...  6.73 us
    convert_element_type x2, other arithmetic, lanes(): jnp.where(row_out | col_out, -1e+30, 0.0).astype(BF).reshape(n * W, 128)  2.92 us
  transfers between devices with their start and end apart: 12, of which 5 were waited for; matrix products, arithmetic and copies ran while one was open for 6% of the time, Pallas kernels for 17%

commit v1 on v0

--- a/solution.py
+++ b/solution.py
@@ -321,13 +321,18 @@
     attended, corr, ds, *dkf = run_far(start, vm, vf, q, gs, pm, pf, linv)
     dkf = from_lat(*dkf)
     grad_queries, mid = run_mid(start, km, kf, vm, q, gs, pm, corr, ds)
-    mid = mid.reshape(2, T, W, 128) + jnp.stack([dkf, dvf])
-    west = mid[:, :, :T].astype(BF)
-    east = mid[:, :, 2 * T :].astype(BF)
-    near = swap(jnp.where(even, east, west), 0)
-    far = swap(jnp.where(even, west, east), 1)
-    grads = [(mid[i, :, T : 2 * T] + near[i].astype(F32) + far[i].astype(F32)).astype(BF) for i in range(2)]
-    return attended.reshape(T, T, 128), grad_queries.reshape(T, T, 128), grads[0], grads[1]
+    mid = mid.reshape(2, T, W, 128)
+
+    def fold_lon(x):
+        west = x[:, :T].astype(BF)
+        east = x[:, 2 * T :].astype(BF)
+        near = swap(jnp.where(even, east, west), 0)
+        far = swap(jnp.where(even, west, east), 1)
+        return (x[:, T : 2 * T] + near.astype(F32) + far.astype(F32)).astype(BF)
+
+    grad_values = fold_lon(mid[1] + dvf)
+    grad_keys = fold_lon(mid[0] + dkf)
+    return attended.reshape(T, T, 128), grad_queries.reshape(T, T, 128), grad_keys, grad_values
 
 
 def solution(mesh):

time: 104 us -> 104 us (level)
  the two profiles are of different devices: /device:TPU:18 before, /device:TPU:15 now
where the time goes in v1:
time: 104 us; the launch traced here: 103 us
  starting transfers between devices  57.3 us (55%)
  Pallas kernels  24.7 us (24%)
  waiting for transfers between devices  10.8 us (10%)
  other arithmetic  8.35 us (8%)
  between operations  1.14 us (1%)
    ppermute x6, starting transfers between devices, swap(): return lax.ppermute(x, 'lon', pairs + [(b, a) for a, b in pairs])  32.1 us
    ppermute x8, starting transfers between devices, shift(): lax.ppermute(x, 'lat', [(i, i + by) for i in range(n) if 0 <= i + by < n])  25.1 us
    ppermute x6, waiting for transfers between devices, swap(): return lax.ppermute(x, 'lon', pairs + [(b, a) for a, b in pairs])  8.4 us
    pallas_call x1, Pallas kernels, run_a(): call(kernel_a, NB + 1, [whole(2 * EDGE, 128), whole(2 * EDGE, 128), per_b...  7.98 us
    pallas_call x1, Pallas kernels, run_far(): call(kernel_far, NB, [whole(MID, 128), whole(2 * EDGE, 128), per_block(NQ...  7.48 us
    pallas_call x1, Pallas kernels, run_mid(): call(kernel_mid, NB, [whole(MID, 128), whole(2 * EDGE, 128), whole(MID, 1...  6.74 us
    convert_element_type x2, other arithmetic, lanes(): jnp.where(row_out | col_out, -1e+30, 0.0).astype(BF).reshape(n * W, 128)  2.92 us
    pallas_call x1, Pallas kernels, run_early(): call(kernel_early, NB, [whole(MID, 128), whole(MID, 128), per_block(NQ, 2...  2.53 us
  transfers between devices with their start and end apart: 14, of which 4 were waited for; matrix products, arithmetic and copies ran while one was open for 7% of the time, Pallas kernels for 24%

profile of v1, /device:TPU:15, one launch (start us, length us, event | category | flops | bytes accessed | tf_op | source)
XLA Modules:
  0.0 103.3 jit_solution(13799805195536661537)
XLA Ops:
  0.6 1.0 pad_maximum_fusion.5
  1.6 4.4 %collective-permute-start = (bf16[2,24,24,128]{3,2,1,0:T(8,128)(2,1)S(1)}, bf16[2,24,24,128]{3,2,1,0:T(8,128)(2,1)S(1)}, u32[]{:S(2)}, u32[]{:S(2)}) collective-permute-start(bf16[2,24,24,128]{3,2,1,0:T(8,128)(2,1)S(1)} %pad_maximum_fusion.5), channel_id=1, source_target_pairs={{1,2},{3,4},{5,6},{7,8},{9,10},{11,12},{13,14},{15,16},{17,18},{19... | collective-permute-start | bytes 884744 | tf_op jit(solution)/shard_map/ppermute | solution.py:285
  6.0 11.3 %collective-permute-start.1 = (bf16[2,24,24,128]{3,2,1,0:T(8,128)(2,1)S(1)}, bf16[2,24,24,128]{3,2,1,0:T(8,128)(2,1)S(1)}, u32[]{:S(2)}, u32[]{:S(2)}) collective-permute-start(bf16[2,24,24,128]{3,2,1,0:T(8,128)(2,1)S(1)} %pad_maximum_fusion.5), channel_id=1, source_target_pairs={{0,1},{2,3},{4,5},{6,7},{8,9},{10,11},{12,13},{14,15},{16,17},{18,... | collective-permute-start | bytes 884744 | tf_op jit(solution)/shard_map/ppermute | solution.py:285
  20.5 1.8 %select_convert_fusion.af_ref = bf16[3168,128]{1,0:T(8,128)(2,1)S(1)} fusion(s32[128]{0:T(128)S(1)} %get-tuple-element.63, s32[128]{0:T(128)S(1)} %get-tuple-element.62, s32[128]{0:T(128)S(1)} %get-tuple-element.55, s32[128]{0:T(128)S(1)} %get-tuple-element.54, s32[3168]{0:T(1024)S(1)} %iota.176, s32[3168]{0:T(1024)S(1)} %add.158, ...), kind=kLoop, calls=%fused_computation | loop fusion | flops 4460544 | bytes 838656 | tf_op jit(solution)/shard_map/convert_element_type | solution.py:255
  22.3 1.1 %select_convert_fusion.1.am_ref = bf16[1728,128]{1,0:T(8,128)(2,1)S(1)} fusion(s32[128]{0:T(128)S(1)} %get-tuple-element.63, s32[128]{0:T(128)S(1)} %get-tuple-element.62, s32[128]{0:T(128)S(1)} %get-tuple-element.55, s32[128]{0:T(128)S(1)} %get-tuple-element.54, s32[1728]{0:T(1024)S(1)} %iota.188, s32[1728]{0:T(1024)S(1)} %add.169, ...), kind=kLoop, calls=%fused_computation.3 | loop fusion | flops 2433024 | bytes 458496 | tf_op jit(solution)/shard_map/convert_element_type | solution.py:255
  23.4 2.1 %collective-permute-done.1 = bf16[2,24,24,128]{3,2,1,0:T(8,128)(2,1)S(1)} collective-permute-done((bf16[2,24,24,128]{3,2,1,0:T(8,128)(2,1)S(1)}, bf16[2,24,24,128]{3,2,1,0:T(8,128)(2,1)S(1)}, u32[]{:S(2)}, u32[]{:S(2)}) %collective-permute-start.1) | collective-permute-done | bytes 294944 | tf_op jit(solution)/shard_map/ppermute | solution.py:285
  25.8 3.8 %collective-permute-start.4 = (bf16[22,72,128]{2,1,0:T(8,128)(2,1)S(1)}, bf16[22,72,128]{2,1,0:T(8,128)(2,1)S(1)}, u32[]{:S(2)}, u32[]{:S(2)}) collective-permute-start(bf16[22,72,128]{2,1,0:T(8,128)(2,1)S(1)} %get-tuple-element.48), channel_id=1, source_target_pairs={{0,32},{32,64},{64,96},{96,128},{128,160},{160,192},{192,224},{224... | collective-permute-start | bytes 1216520 | tf_op jit(solution)/shard_map/ppermute | solution.py:279
  29.7 1.9 %collective-permute-start.5 = (bf16[22,72,128]{2,1,0:T(8,128)(2,1)S(1)}, bf16[22,72,128]{2,1,0:T(8,128)(2,1)S(1)}, u32[]{:S(2)}, u32[]{:S(2)}) collective-permute-start(bf16[22,72,128]{2,1,0:T(8,128)(2,1)S(1)} %get-tuple-element.49), channel_id=1, source_target_pairs={{32,0},{64,32},{96,64},{128,96},{160,128},{192,160},{224,192},{256... | collective-permute-start | bytes 1216520 | tf_op jit(solution)/shard_map/ppermute | solution.py:279
  31.7 4.5 %collective-permute-start.2 = (bf16[22,72,128]{2,1,0:T(8,128)(2,1)S(1)}, bf16[22,72,128]{2,1,0:T(8,128)(2,1)S(1)}, u32[]{:S(2)}, u32[]{:S(2)}) collective-permute-start(bf16[22,72,128]{2,1,0:T(8,128)(2,1)S(1)} %get-tuple-element.50), channel_id=1, source_target_pairs={{0,32},{32,64},{64,96},{96,128},{128,160},{160,192},{192,224},{224... | collective-permute-start | bytes 1216520 | tf_op jit(solution)/shard_map/ppermute | solution.py:279
  36.3 1.9 %collective-permute-start.3 = (bf16[22,72,128]{2,1,0:T(8,128)(2,1)S(1)}, bf16[22,72,128]{2,1,0:T(8,128)(2,1)S(1)}, u32[]{:S(2)}, u32[]{:S(2)}) collective-permute-start(bf16[22,72,128]{2,1,0:T(8,128)(2,1)S(1)} %get-tuple-element.51), channel_id=1, source_target_pairs={{32,0},{64,32},{96,64},{128,96},{160,128},{192,160},{224,192},{256... | collective-permute-start | bytes 1216520 | tf_op jit(solution)/shard_map/ppermute | solution.py:279
  38.2 2.5 %shard_map.75 = (f32[3,1728,384]{2,1,0:T(8,128)S(1)}, f32[3,8,384]{2,1,0:T(8,128)S(1)}) custom-call(s32[3]{0:T(128)S(1)} %fusion.5.start, bf16[1728,128]{1,0:T(8,128)(2,1)S(1)} %bitcast.31, bf16[1728,128]{1,0:T(8,128)(2,1)S(1)} %select_convert_fusion.1.am_ref, bf16[3,384,256]{2,1,0:T(8,128)(2,1)S(1)} %pad_maximum_fusion.2.q_ref), custom_call_target="tpu_custom_call" | custom-call | flops 1000000000 | bytes 14000000 | tf_op jit(solution)/shard_map/pallas_call | solution.py:190
  40.8 2.4 %collective-permute-done.5 = bf16[22,72,128]{2,1,0:T(8,128)(2,1)S(1)} collective-permute-done((bf16[22,72,128]{2,1,0:T(8,128)(2,1)S(1)}, bf16[22,72,128]{2,1,0:T(8,128)(2,1)S(1)}, u32[]{:S(2)}, u32[]{:S(2)}) %collective-permute-start.5) | collective-permute-done | bytes 405536 | tf_op jit(solution)/shard_map/ppermute | solution.py:279
  43.2 8.0 %shard_map.76 = (bf16[3,1728,384]{2,1,0:T(8,128)(2,1)S(1)}, bf16[3,2016,384]{2,1,0:T(8,128)(2,1)S(1)}, f32[3,8,384]{2,1,0:T(8,128)S(1)}, bf16[3,384,128]{2,1,0:T...) custom-call(s32[3]{0:T(128)S(1)} %fusion.5.start, bf16[3168,128]{1,0:T(8,128)(2,1)S(1)} %bitcast.33, ...), custom_call_target="tpu_custom_call" | custom-call | flops 5000000000 | bytes 14000000 | tf_op jit(solution)/shard_map/pallas_call | solution.py:204
  51.2 1.9 %collective-permute-start.10 = (bf16[1584,128]{1,0:T(8,128)(2,1)S(1)}, bf16[1584,128]{1,0:T(8,128)(2,1)S(1)}, u32[]{:S(2)}, u32[]{:S(2)}) collective-permute-start(bf16[1584,128]{1,0:T(8,128)(2,1)S(1)} %get-tuple-element.32), channel_id=1, source_target_pairs={{32,0},{64,32},{96,64},{128,96},{160,128},{192,160},{224,192},{256... | collective-permute-start | bytes 1216520 | tf_op jit(solution)/shard_map/ppermute | solution.py:279
  53.2 4.5 %collective-permute-start.11 = (bf16[1584,128]{1,0:T(8,128)(2,1)S(1)}, bf16[1584,128]{1,0:T(8,128)(2,1)S(1)}, u32[]{:S(2)}, u32[]{:S(2)}) collective-permute-start(bf16[1584,128]{1,0:T(8,128)(2,1)S(1)} %get-tuple-element.33), channel_id=1, source_target_pairs={{0,32},{32,64},{64,96},{96,128},{128,160},{160,192},{192,224},{224... | collective-permute-start | bytes 1216520 | tf_op jit(solution)/shard_map/ppermute | solution.py:279
  57.8 7.5 %shard_map.77 = (bf16[576,128]{1,0:T(8,128)(2,1)}, f32[3,8,384]{2,1,0:T(8,128)S(1)}, bf16[3,2016,384]{2,1,0:T(8,128)(2,1)S(1)}, bf16[1584,128]{1,0:T(8,128)(2,1)S(1)}, bf16[1584,128]{1,0:T(8,128)(2,1)S(1)}) custom-call(s32[3]{0:T(128)S(1)} %fusion.5.start, bf16[1728,128]{1,0:T(8,128)(2,1)S(1)} %bitcast.29, bf16[3168,128]{1,0:T(8,128)(2,1)S(1)} %bitcast.35, ...), custom_call_target="tpu_custom_call" | custom-call | flops 5000000000 | bytes 14000000 | tf_op jit(solution)/shard_map/pallas_call | solution.py:217
  65.3 1.9 %collective-permute-start.6 = (bf16[1584,128]{1,0:T(8,128)(2,1)S(1)}, bf16[1584,128]{1,0:T(8,128)(2,1)S(1)}, u32[]{:S(2)}, u32[]{:S(2)}) collective-permute-start(bf16[1584,128]{1,0:T(8,128)(2,1)S(1)} %get-tuple-element.30), channel_id=1, source_target_pairs={{32,0},{64,32},{96,64},{128,96},{160,128},{192,160},{224,192},{256... | collective-permute-start | bytes 1216520 | tf_op jit(solution)/shard_map/ppermute | solution.py:279
  67.2 4.5 %collective-permute-start.7 = (bf16[1584,128]{1,0:T(8,128)(2,1)S(1)}, bf16[1584,128]{1,0:T(8,128)(2,1)S(1)}, u32[]{:S(2)}, u32[]{:S(2)}) collective-permute-start(bf16[1584,128]{1,0:T(8,128)(2,1)S(1)} %get-tuple-element.31), channel_id=1, source_target_pairs={{0,32},{32,64},{64,96},{96,128},{128,160},{160,192},{192,224},{224... | collective-permute-start | bytes 1216520 | tf_op jit(solution)/shard_map/ppermute | solution.py:279
  71.8 6.7 %shard_map.78 = (bf16[576,128]{1,0:T(8,128)(2,1)}, f32[2,1728,128]{2,1,0:T(8,128)S(1)}) custom-call(s32[3]{0:T(128)S(1)} %fusion.5.start, bf16[1728,128]{1,0:T(8,128)(2,1)S(1)} %bitcast.32, bf16[3168,128]{1,0:T(8,128)(2,1)S(1)} %bitcast.34, bf16[1728,128]{1,0:T(8,128)(2,1)S(1)} %bitcast.30, bf16[3,384,256]{2,1,0:T(8,128)(2,1)S(1)} %pad_maximum_fusion.2.q_ref, ...), custom_call_target="tpu_custom_call" | custom-call | flops 5000000000 | bytes 14000000 | tf_op jit(solution)/shard_map/pallas_call | solution.py:230
  78.8 6.0 %collective-permute-start.12 = (bf16[24,24,128]{2,1,0:T(8,128)(2,1)S(1)}, bf16[24,24,128]{2,1,0:T(8,128)(2,1)S(1)}, u32[]{:S(2)}, u32[]{:S(2)}) collective-permute-start(bf16[24,24,128]{2,1,0:T(8,128)(2,1)S(1)} %get-tuple-element.44), channel_id=1, source_target_pairs={{0,1},{2,3},{4,5},{6,7},{8,9},{10,11},{12,13},{14,15},{16,17},{18,... | collective-permute-start | bytes 442376 | tf_op jit(solution)/shard_map/ppermute | solution.py:285
  84.9 1.9 %collective-permute-start.13 = (bf16[24,24,128]{2,1,0:T(8,128)(2,1)S(1)}, bf16[24,24,128]{2,1,0:T(8,128)(2,1)S(1)}, u32[]{:S(2)}, u32[]{:S(2)}) collective-permute-start(bf16[24,24,128]{2,1,0:T(8,128)(2,1)S(1)} %get-tuple-element.45), channel_id=1, source_target_pairs={{1,2},{3,4},{5,6},{7,8},{9,10},{11,12},{13,14},{15,16},{17,18},{19... | collective-permute-start | bytes 442376 | tf_op jit(solution)/shard_map/ppermute | solution.py:285
  87.0 6.6 %collective-permute-start.8 = (bf16[24,24,128]{2,1,0:T(8,128)(2,1)S(1)}, bf16[24,24,128]{2,1,0:T(8,128)(2,1)S(1)}, u32[]{:S(2)}, u32[]{:S(2)}) collective-permute-start(bf16[24,24,128]{2,1,0:T(8,128)(2,1)S(1)} %get-tuple-element.46), channel_id=1, source_target_pairs={{0,1},{2,3},{4,5},{6,7},{8,9},{10,11},{12,13},{14,15},{16,17},{18,... | collective-permute-start | bytes 442376 | tf_op jit(solution)/shard_map/ppermute | solution.py:285
  93.6 1.9 %collective-permute-start.9 = (bf16[24,24,128]{2,1,0:T(8,128)(2,1)S(1)}, bf16[24,24,128]{2,1,0:T(8,128)(2,1)S(1)}, u32[]{:S(2)}, u32[]{:S(2)}) collective-permute-start(bf16[24,24,128]{2,1,0:T(8,128)(2,1)S(1)} %get-tuple-element.47), channel_id=1, source_target_pairs={{1,2},{3,4},{5,6},{7,8},{9,10},{11,12},{13,14},{15,16},{17,18},{19... | collective-permute-start | bytes 442376 | tf_op jit(solution)/shard_map/ppermute | solution.py:285
  96.5 6.0 %collective-permute-done.9 = bf16[24,24,128]{2,1,0:T(8,128)(2,1)S(1)} collective-permute-done((bf16[24,24,128]{2,1,0:T(8,128)(2,1)S(1)}, bf16[24,24,128]{2,1,0:T(8,128)(2,1)S(1)}, u32[]{:S(2)}, u32[]{:S(2)}) %collective-permute-start.9) | collective-permute-done | bytes 147488 | tf_op jit(solution)/shard_map/ppermute | solution.py:285
  (56 shorter events, 5.6 us)
Async XLA Ops:
  1.6 21.8 %collective-permute-start = (bf16[2,24,24,128]{3,2,1,0:T(8,128)(2,1)S(1)}, bf16[2,24,24,128]{3,2,1,0:T(8,128)(2,1)S(1)}, u32[]{:S(2)}, u32[]{:S(2)}) collective-permute-start(bf16[2,24,24,128]{3,2,1,0:T(8,128)(2,1)S(1)} %pad_maximum_fusion.5), channel_id=1, source_target_pairs={{1,2},{3,4},{5,6},{7,8},{9,10},{11,12},{13,14},{15,16},{17,18},{19... | collective-permute-start | bytes 884744 | tf_op jit(solution)/shard_map/ppermute | solution.py:285
  6.0 19.5 %collective-permute-start.1 = (bf16[2,24,24,128]{3,2,1,0:T(8,128)(2,1)S(1)}, bf16[2,24,24,128]{3,2,1,0:T(8,128)(2,1)S(1)}, u32[]{:S(2)}, u32[]{:S(2)}) collective-permute-start(bf16[2,24,24,128]{3,2,1,0:T(8,128)(2,1)S(1)} %pad_maximum_fusion.5), channel_id=1, source_target_pairs={{0,1},{2,3},{4,5},{6,7},{8,9},{10,11},{12,13},{14,15},{16,17},{18,... | collective-permute-start | bytes 884744 | tf_op jit(solution)/shard_map/ppermute | solution.py:285
  20.4 5.2 %copy-start = (bf16[24,24,128]{2,1,0:T(8,128)(2,1)S(1)}, bf16[24,24,128]{2,1,0:T(8,128)(2,1)}, u32[]{:S(2)}) copy-start(bf16[24,24,128]{2,1,0:T(8,128)(2,1)} %param.6) | copy-start | bytes 442372
  20.4 5.2 %copy-start.1 = (bf16[24,24,128]{2,1,0:T(8,128)(2,1)S(1)}, bf16[24,24,128]{2,1,0:T(8,128)(2,1)}, u32[]{:S(2)}) copy-start(bf16[24,24,128]{2,1,0:T(8,128)(2,1)} %param.5) | copy-start | bytes 442372
  25.8 14.9 %collective-permute-start.4 = (bf16[22,72,128]{2,1,0:T(8,128)(2,1)S(1)}, bf16[22,72,128]{2,1,0:T(8,128)(2,1)S(1)}, u32[]{:S(2)}, u32[]{:S(2)}) collective-permute-start(bf16[22,72,128]{2,1,0:T(8,128)(2,1)S(1)} %get-tuple-element.48), channel_id=1, source_target_pairs={{0,32},{32,64},{64,96},{96,128},{128,160},{160,192},{192,224},{224... | collective-permute-start | bytes 1216520 | tf_op jit(solution)/shard_map/ppermute | solution.py:279
  29.7 13.5 %collective-permute-start.5 = (bf16[22,72,128]{2,1,0:T(8,128)(2,1)S(1)}, bf16[22,72,128]{2,1,0:T(8,128)(2,1)S(1)}, u32[]{:S(2)}, u32[]{:S(2)}) collective-permute-start(bf16[22,72,128]{2,1,0:T(8,128)(2,1)S(1)} %get-tuple-element.49), channel_id=1, source_target_pairs={{32,0},{64,32},{96,64},{128,96},{160,128},{192,160},{224,192},{256... | collective-permute-start | bytes 1216520 | tf_op jit(solution)/shard_map/ppermute | solution.py:279
  31.7 26.0 %collective-permute-start.2 = (bf16[22,72,128]{2,1,0:T(8,128)(2,1)S(1)}, bf16[22,72,128]{2,1,0:T(8,128)(2,1)S(1)}, u32[]{:S(2)}, u32[]{:S(2)}) collective-permute-start(bf16[22,72,128]{2,1,0:T(8,128)(2,1)S(1)} %get-tuple-element.50), channel_id=1, source_target_pairs={{0,32},{32,64},{64,96},{96,128},{128,160},{160,192},{192,224},{224... | collective-permute-start | bytes 1216520 | tf_op jit(solution)/shard_map/ppermute | solution.py:279
  36.3 21.5 %collective-permute-start.3 = (bf16[22,72,128]{2,1,0:T(8,128)(2,1)S(1)}, bf16[22,72,128]{2,1,0:T(8,128)(2,1)S(1)}, u32[]{:S(2)}, u32[]{:S(2)}) collective-permute-start(bf16[22,72,128]{2,1,0:T(8,128)(2,1)S(1)} %get-tuple-element.51), channel_id=1, source_target_pairs={{32,0},{64,32},{96,64},{128,96},{160,128},{192,160},{224,192},{256... | collective-permute-start | bytes 1216520 | tf_op jit(solution)/shard_map/ppermute | solution.py:279
  51.2 27.4 %collective-permute-start.10 = (bf16[1584,128]{1,0:T(8,128)(2,1)S(1)}, bf16[1584,128]{1,0:T(8,128)(2,1)S(1)}, u32[]{:S(2)}, u32[]{:S(2)}) collective-permute-start(bf16[1584,128]{1,0:T(8,128)(2,1)S(1)} %get-tuple-element.32), channel_id=1, source_target_pairs={{32,0},{64,32},{96,64},{128,96},{160,128},{192,160},{224,192},{256... | collective-permute-start | bytes 1216520 | tf_op jit(solution)/shard_map/ppermute | solution.py:279
  53.2 25.5 %collective-permute-start.11 = (bf16[1584,128]{1,0:T(8,128)(2,1)S(1)}, bf16[1584,128]{1,0:T(8,128)(2,1)S(1)}, u32[]{:S(2)}, u32[]{:S(2)}) collective-permute-start(bf16[1584,128]{1,0:T(8,128)(2,1)S(1)} %get-tuple-element.33), channel_id=1, source_target_pairs={{0,32},{32,64},{64,96},{96,128},{128,160},{160,192},{192,224},{224... | collective-permute-start | bytes 1216520 | tf_op jit(solution)/shard_map/ppermute | solution.py:279
  65.3 21.5 %collective-permute-start.6 = (bf16[1584,128]{1,0:T(8,128)(2,1)S(1)}, bf16[1584,128]{1,0:T(8,128)(2,1)S(1)}, u32[]{:S(2)}, u32[]{:S(2)}) collective-permute-start(bf16[1584,128]{1,0:T(8,128)(2,1)S(1)} %get-tuple-element.30), channel_id=1, source_target_pairs={{32,0},{64,32},{96,64},{128,96},{160,128},{192,160},{224,192},{256... | collective-permute-start | bytes 1216520 | tf_op jit(solution)/shard_map/ppermute | solution.py:279
  67.2 19.6 %collective-permute-start.7 = (bf16[1584,128]{1,0:T(8,128)(2,1)S(1)}, bf16[1584,128]{1,0:T(8,128)(2,1)S(1)}, u32[]{:S(2)}, u32[]{:S(2)}) collective-permute-start(bf16[1584,128]{1,0:T(8,128)(2,1)S(1)} %get-tuple-element.31), channel_id=1, source_target_pairs={{0,32},{32,64},{64,96},{96,128},{128,160},{160,192},{192,224},{224... | collective-permute-start | bytes 1216520 | tf_op jit(solution)/shard_map/ppermute | solution.py:279
  78.8 16.7 %collective-permute-start.12 = (bf16[24,24,128]{2,1,0:T(8,128)(2,1)S(1)}, bf16[24,24,128]{2,1,0:T(8,128)(2,1)S(1)}, u32[]{:S(2)}, u32[]{:S(2)}) collective-permute-start(bf16[24,24,128]{2,1,0:T(8,128)(2,1)S(1)} %get-tuple-element.44), channel_id=1, source_target_pairs={{0,1},{2,3},{4,5},{6,7},{8,9},{10,11},{12,13},{14,15},{16,17},{18,... | collective-permute-start | bytes 442376 | tf_op jit(solution)/shard_map/ppermute | solution.py:285
  84.9 10.7 %collective-permute-start.13 = (bf16[24,24,128]{2,1,0:T(8,128)(2,1)S(1)}, bf16[24,24,128]{2,1,0:T(8,128)(2,1)S(1)}, u32[]{:S(2)}, u32[]{:S(2)}) collective-permute-start(bf16[24,24,128]{2,1,0:T(8,128)(2,1)S(1)} %get-tuple-element.45), channel_id=1, source_target_pairs={{1,2},{3,4},{5,6},{7,8},{9,10},{11,12},{13,14},{15,16},{17,18},{19... | collective-permute-start | bytes 442376 | tf_op jit(solution)/shard_map/ppermute | solution.py:285
  87.0 9.5 %collective-permute-start.8 = (bf16[24,24,128]{2,1,0:T(8,128)(2,1)S(1)}, bf16[24,24,128]{2,1,0:T(8,128)(2,1)S(1)}, u32[]{:S(2)}, u32[]{:S(2)}) collective-permute-start(bf16[24,24,128]{2,1,0:T(8,128)(2,1)S(1)} %get-tuple-element.46), channel_id=1, source_target_pairs={{0,1},{2,3},{4,5},{6,7},{8,9},{10,11},{12,13},{14,15},{16,17},{18,... | collective-permute-start | bytes 442376 | tf_op jit(solution)/shard_map/ppermute | solution.py:285
  93.6 9.0 %collective-permute-start.9 = (bf16[24,24,128]{2,1,0:T(8,128)(2,1)S(1)}, bf16[24,24,128]{2,1,0:T(8,128)(2,1)S(1)}, u32[]{:S(2)}, u32[]{:S(2)}) collective-permute-start(bf16[24,24,128]{2,1,0:T(8,128)(2,1)S(1)} %get-tuple-element.47), channel_id=1, source_target_pairs={{1,2},{3,4},{5,6},{7,8},{9,10},{11,12},{13,14},{15,16},{17,18},{19... | collective-permute-start | bytes 442376 | tf_op jit(solution)/shard_map/ppermute | solution.py:285
